TPU v7x, 32 devices: a whole 2x2x4 slice. The times are simulated.
32 devices in a mesh: groups: 2 (over x), hid: 8 (over z, y), wid: 2 (over core).
Axes of the slice: x: 2, y: 2, z: 4, core: 2. Of those that a mesh axis runs over, the one named last changes fastest.
Arguments:
- tokens: bfloat16 [256, 18432], P(('groups', 'hid'), 'wid'), parts along dimension 0, may hold values from -180 to 180
- norm_gain: float32 [18432], P('wid'), may hold values from 0.1 to 1.9
- query_weight: bfloat16 [18432, 8192], P('wid', 'hid'), may hold values from -0.046875 to 0.046875
- query_scale: float32 [8192], P('hid'), may hold values from 0.5 to 2
- kv_weight: bfloat16 [18432, 512], P('wid'), may hold values from -0.046875 to 0.046875
- kv_scale: float32 [512], replicated, may hold values from 0.5 to 2
- keys_cache: bfloat16 [256, 512, 256], P(('groups', 'hid', 'wid')), parts along dimension 0, may hold values from -384 to 384
- values_cache: bfloat16 [256, 512, 256], P(('groups', 'hid', 'wid')), parts along dimension 0, may hold values from -6 to 6
- lengths: int32 [256], P(('groups', 'hid', 'wid')), parts along dimension 0, may hold values from 1 to 512, as said below
Outputs:
- attended: bfloat16 [256, 8192], P(('groups', 'hid', 'wid')), parts along dimension 0
- new_entries: bfloat16 [256, 512], P(('groups', 'hid', 'wid')), parts along dimension 0
There are 2 independent parts, one for each index of `groups`. A program takes and returns all parts, laid end to end along the dimension named above; an argument that names none is the same for every part. Nothing has to cross between parts.
Inputs may be any that keep to these rules, and one draw needn't show every extreme that they name: `lengths`: in one aligned block of 8 requests every length is 512.
All inputs are finite; a program needn't handle non-finite values.
Results may differ from a plain program's by a relative error of at most 0.009.
The roundings to bfloat16 on the way count: a program that leaves them out, or rounds other values in their place, can miss the bound.
Values may be sent and summed in bfloat16 or wider, within the bound.
A program may use at most 128 MiB of HBM per device.

v0:
```python
import jax
import jax.numpy as jnp
from jax import lax
from jax.sharding import PartitionSpec as P

EPSILON = 1e-05


def layer_norm(row_values, row_sum, row_squares, full_width, gain_f32):
    row_mean = row_sum / full_width
    variance = row_squares / full_width - row_mean * row_mean
    return (
        (row_values - row_mean[:, None]) * lax.rsqrt(variance + EPSILON)[:, None] * gain_f32
    ).astype(jnp.bfloat16)


def attend_local(queries, new_entries, keys_cache, values_cache, lengths):
    row_count, cache_len, head_dim = keys_cache.shape
    head_count = queries.shape[1] // head_dim
    query_heads = queries.reshape(row_count, head_count, head_dim)
    new_keys = new_entries[:, :head_dim]
    new_values = new_entries[:, head_dim:]
    inv_root = head_dim ** (-0.5)
    cache_scores = (
        jnp.einsum("rhd,rtd->rht", query_heads, keys_cache, preferred_element_type=jnp.float32)
        * inv_root
    )
    positions = lax.broadcasted_iota(jnp.int32, (row_count, 1, cache_len), 2)
    is_live = positions < lengths[:, None, None]
    cache_scores = jnp.where(is_live, cache_scores, -jnp.inf)
    own_scores = (
        jnp.einsum("rhd,rd->rh", query_heads, new_keys, preferred_element_type=jnp.float32)
        * inv_root
    )
    peak_score = jnp.maximum(jnp.max(cache_scores, axis=2), own_scores)
    cache_exp = jnp.exp(cache_scores - peak_score[:, :, None])
    own_exp = jnp.exp(own_scores - peak_score)
    denom_sum = jnp.sum(cache_exp, axis=2) + own_exp
    cache_weights = (cache_exp / denom_sum[:, :, None]).astype(jnp.bfloat16)
    own_weights = (own_exp / denom_sum).astype(jnp.bfloat16)
    blended = jnp.einsum(
        "rht,rtd->rhd", cache_weights, values_cache, preferred_element_type=jnp.float32
    )
    blended = (
        blended
        + own_weights.astype(jnp.float32)[:, :, None] * new_values.astype(jnp.float32)[:, None, :]
    )
    return blended.reshape(row_count, head_count * head_dim).astype(jnp.bfloat16)


def body(
    tokens,
    norm_gain,
    query_weight,
    query_scale,
    kv_weight,
    kv_scale,
    keys_cache,
    values_cache,
    lengths,
):
    hid_count = lax.axis_size("hid")
    wid_count = lax.axis_size("wid")
    full_width = tokens.shape[1] * wid_count
    own_rows = tokens.shape[0]
    gathered = lax.all_gather(tokens, "hid", axis=0, tiled=True)
    row_values = gathered.astype(jnp.float32)
    row_sum, row_squares = lax.psum(
        (jnp.sum(row_values, axis=1), jnp.sum(row_values * row_values, axis=1)), "wid"
    )
    all_normed = layer_norm(row_values, row_sum, row_squares, full_width, norm_gain)
    query_part = jnp.dot(all_normed, query_weight, preferred_element_type=jnp.float32) * query_scale
    own_normed = lax.dynamic_slice_in_dim(all_normed, lax.axis_index("hid") * own_rows, own_rows, 0)
    entry_part = jnp.dot(own_normed, kv_weight, preferred_element_type=jnp.float32) * kv_scale
    entry_sum = lax.psum_scatter(
        entry_part.astype(jnp.bfloat16), "wid", scatter_dimension=0, tiled=True
    )
    local_cols = query_part.shape[1]
    attend_rows = own_rows // wid_count
    halves = query_part.reshape(hid_count, wid_count, attend_rows, local_cols)
    summed = lax.psum_scatter(halves, "wid", scatter_dimension=1, tiled=True)
    rounded = summed.reshape(hid_count, attend_rows, local_cols).astype(jnp.bfloat16)
    swapped = lax.all_to_all(rounded, "hid", split_axis=0, concat_axis=2, tiled=True)
    queries = swapped.reshape(attend_rows, hid_count * local_cols)
    attended = attend_local(queries, entry_sum, keys_cache, values_cache, lengths)
    return (attended, entry_sum)


def solution(mesh):
    placed = (
        P(("groups", "hid"), "wid"),
        P("wid"),
        P("wid", "hid"),
        P("hid"),
        P("wid", None),
        P(),
        P(("groups", "hid", "wid"), None, None),
        P(("groups", "hid", "wid"), None, None),
        P(("groups", "hid", "wid")),
    )
    return jax.shard_map(
        body,
        mesh=mesh,
        in_specs=placed,
        out_specs=(P(("groups", "hid", "wid"), None), P(("groups", "hid", "wid"), None)),
        check_vma=False,
    )
```

profile of v0, /device:TPU:0, one launch (start us, length us, event | category | flops | bytes accessed | tf_op | source)
XLA Modules:
  0.0 114.9 jit_solution(10334993035902951413)
XLA Ops:
  7.2 0.7 all-gather.2.cloned.1.call-update
  7.9 0.0 reduce-scatter.3.cloned.1.call-start
  8.0 1.3 %dynamic-slice = u32[1]{0:T(128)} dynamic-slice(u32[32]{0:T(128)} %constant.30, u32[]{:T(128)S(6)} %add.29), dynamic_slice_sizes={1} | dynamic-slice | bytes 12
  9.3 55.5 %all-gather.2.cloned.1.call-done = bf16[128,9216]{1,0:T(8,128)(2,1)} async-done(((bf16[16,9216]{1,0:T(8,128)(2,1)}), bf16[128,9216]{1,0:T(8,128)(2,1)}) %all-gather.2.cloned.1.call-update) | async-done | bytes 2359312 | tf_op jit(solution)/shard_map/all_gather | solution.py:66
  64.8 2.4 %convert_reduce_fusion = (f32[128]{0:T(128)S(1)}, f32[128]{0:T(128)S(1)}) fusion(bf16[128,9216]{1,0:T(8,128)(2,1)} %all-gather.2.cloned.1.call-done), kind=kLoop, calls=%fused_computation.2 | loop fusion | flops 4718336 | bytes 2360320 | tf_op jit(solution)/shard_map/reduce_sum | solution.py:69
  67.1 2.5 %all-reduce.1 = (f32[128]{0:T(128)S(1)}, f32[128]{0:T(128)S(1)}) all-reduce(f32[128]{0:T(128)S(1)} %get-tuple-element.3, f32[128]{0:T(128)S(1)} %get-tuple-element.2), channel_id=1, replica_groups=mesh['groups'=2,'hid'=8,'wid'=2] {'wid'}, use_global_device_ids=true, to_apply=%region_3.0 | all-reduce | flops 256 | bytes 2048 | tf_op jit(solution)/shard_map/psum | solution.py:68
  69.6 2.5 %fusion.2 = bf16[128,9216]{1,0:T(8,128)(2,1)S(1)} fusion(bf16[128,9216]{1,0:T(8,128)(2,1)} %all-gather.2.cloned.1.call-done, f32[9216]{0:T(1024)S(1)} %copy-done.2, f32[128]{0:T(128)S(1)} %get-tuple-element.11, f32[128]{0:T(128)S(1)} %get-tuple-element.10), kind=kLoop, calls=%fused_computation.5 | loop fusion | flops 5898240 | bytes 4756480 | tf_op jit(solution)/shard_map/convert_element_type | solution.py:14
  72.1 1.4 %copy-done.1 = bf16[128,9216]{1,0:T(8,128)(2,1)} copy-done((bf16[128,9216]{1,0:T(8,128)(2,1)}, bf16[128,9216]{1,0:T(8,128)(2,1)S(1)}, u32[]{:S(2)}) %copy-start.1) | copy-done | bytes 2359320
  73.5 5.6 %fusion.7 = bf16[16,512]{1,0:T(8,128)(2,1)} fusion(bf16[9216,512]{1,0:T(8,128)(2,1)} %param.13, bf16[128,9216]{1,0:T(8,128)(2,1)S(1)} %fusion.2, s32[]{:T(128)S(6)} %select_n.8, f32[512]{0:T(512)S(1)} %copy-done.4), kind=kOutput, calls=%fused_computation.14 | convolution fusion | flops 151011328 | bytes 9750532 | tf_op jit(solution)/shard_map/dot_general | solution.py:74
  79.2 8.5 %convolution_multiply_fusion.1 = f32[128,1024]{1,0:T(8,128)S(1)} fusion(bf16[128,9216]{1,0:T(8,128)(2,1)} %copy-done.1, bf16[9216,1024]{1,0:T(8,128)(2,1)} %param.11, f32[1024]{0:T(1024)S(1)} %copy-done.3), kind=kOutput, calls=%fused_computation.9 | convolution fusion | flops 2416050176 | bytes 21762048 | tf_op jit(solution)/shard_map/dot_general | solution.py:72
  87.7 4.9 %all-reduce.3 = bf16[8,2,8,1024]{3,2,1,0:T(8,128)(2,1)S(1)} all-reduce(f32[8,2,8,1024]{3,2,1,0:T(8,128)S(1)} %bitcast.25), channel_id=2, replica_groups=mesh['groups'=2,'hid'=8,'wid'=2] {'wid'}, use_global_device_ids=true, to_apply=%region_4.0.clone | all-reduce | flops 131072 | bytes 786432
  92.6 1.4 %fusion.12 = bf16[8,8,1024]{2,1,0:T(8,128)(2,1)} fusion(bf16[8,2,8,1024]{3,2,1,0:T(8,128)(2,1)S(1)} %all-reduce.3, u32[]{:T(128)} %bitcast.9), kind=kLoop, calls=%fused_computation.22 | loop fusion | bytes 262148 | tf_op jit(solution)/shard_map/convert_element_type | solution.py:82
  93.9 3.4 %all-to-all-start = ((bf16[8,8,1024]{2,1,0:T(8,128)(2,1)}), bf16[8,8,1024]{2,1,0:T(8,128)(2,1)S(1)}, u32[]{:S(2)}, u32[]{:S(2)}) async-start(bf16[8,8,1024]{2,1,0:T(8,128)(2,1)} %fusion.12), calls=%async_computation | async-start | bytes 262144 | tf_op jit(solution)/shard_map/all_to_all | solution.py:83
  97.3 0.1 iota_compare_fusion
  97.4 0.7 slice_convert_fusion
  98.1 6.9 %all-to-all-done = bf16[8,8,1024]{2,1,0:T(8,128)(2,1)S(1)} async-done(((bf16[8,8,1024]{2,1,0:T(8,128)(2,1)}), bf16[8,8,1024]{2,1,0:T(8,128)(2,1)S(1)}, u32[]{:S(2)}, u32[]{:S(2)}) %all-to-all-start) | async-done | bytes 131104 | tf_op jit(solution)/shard_map/all_to_all | solution.py:83
  105.0 0.1 copy.12
  105.1 0.1 reshape_reshape.3
  105.2 0.1 fusion.13
  105.3 0.8 fusion.18
  106.2 0.2 fusion.8
  106.4 0.4 copy-done.6
  106.8 0.5 fusion.6
  107.3 0.7 copy.17
  (18 shorter events, 0.1 us)
Async XLA Ops:
  7.2 98.2 %copy-start = (bf16[8,512,256]{2,1,0:T(8,128)(2,1)S(1)}, bf16[8,512,256]{2,1,0:T(8,128)(2,1)}, u32[]{:S(2)}) copy-start(bf16[8,512,256]{2,1,0:T(8,128)(2,1)} %param.15) | copy-start | bytes 6291460
  7.2 62.4 %copy-start.2 = (f32[9216]{0:T(1024)S(1)}, f32[9216]{0:T(1024)}, u32[]{:S(2)}) copy-start(f32[9216]{0:T(1024)} %param.10) | copy-start | bytes 110596
  7.2 57.6 %all-gather.2.cloned.1.call-start = ((), (), s32[]{:S(2)}) async-start(), calls=%async_computation.2 | async-start | bytes 2654208 | tf_op jit(solution)/shard_map/all_gather | solution.py:66
  7.9 89.5 %reduce-scatter.3.cloned.1.call-start = ((), (), s32[]{:S(2)}) async-start(), calls=%async_computation.3 | async-start | bytes 24576 | tf_op jit(solution)/shard_map/reduce_scatter | solution.py:75
  69.6 3.9 %copy-start.4 = (f32[512]{0:T(512)S(1)}, f32[512]{0:T(512)}, u32[]{:S(2)}) copy-start(f32[512]{0:T(512)} %param.14) | copy-start | bytes 6148
  72.1 1.4 %copy-start.1 = (bf16[128,9216]{1,0:T(8,128)(2,1)}, bf16[128,9216]{1,0:T(8,128)(2,1)S(1)}, u32[]{:S(2)}) copy-start(bf16[128,9216]{1,0:T(8,128)(2,1)S(1)} %fusion.2) | copy-start | bytes 7077892
  73.5 5.7 %copy-start.3 = (f32[1024]{0:T(1024)S(1)}, f32[1024]{0:T(1024)}, u32[]{:S(2)}) copy-start(f32[1024]{0:T(1024)} %param.12) | copy-start | bytes 12292
  79.2 18.1 %copy-start.5 = (s32[8]{0:T(128)S(1)}, s32[8]{0:T(128)}, u32[]{:S(2)}) copy-start(s32[8]{0:T(128)} %param.17) | copy-start | bytes 100
  93.9 11.1 %all-to-all-start = ((bf16[8,8,1024]{2,1,0:T(8,128)(2,1)}), bf16[8,8,1024]{2,1,0:T(8,128)(2,1)S(1)}, u32[]{:S(2)}, u32[]{:S(2)}) async-start(bf16[8,8,1024]{2,1,0:T(8,128)(2,1)} %fusion.12), calls=%async_computation | async-start | bytes 262144 | tf_op jit(solution)/shard_map/all_to_all | solution.py:83
  105.2 1.6 %copy-start.6 = (bf16[8,512,256]{2,1,0:T(8,128)(2,1)S(1)}, bf16[8,512,256]{2,1,0:T(8,128)(2,1)}, u32[]{:S(2)}) copy-start(bf16[8,512,256]{2,1,0:T(8,128)(2,1)} %param.16) | copy-start | bytes 6291460
Sparse Core Ops, SparseCore 0:
  10.2 54.5 all-gather.1
  79.3 6.0 reduce-scatter.2
where the time goes:
time: 115 us
  waiting for transfers between devices  63.1 us (55%)
  matrix products  15.6 us (14%)
  between operations  14.2 us (12%)
  blocking collectives  7.32 us (6%)
  other arithmetic  5.88 us (5%)
  local copies, waits for them, and re-layouts  5.37 us (5%)
  starting transfers between devices  3.45 us (3%)
    all_gather x1, waiting for transfers between devices, body(): gathered = lax.all_gather(tokens, 'hid', axis=0, tiled=True)  55.5 us
    dot_general x1, matrix products, body(): jnp.dot(all_normed, query_weight, preferred_element_type=jnp.float32)  8.51 us
    all_to_all x1, waiting for transfers between devices, body(): lax.all_to_all(rounded, 'hid', split_axis=0, concat_axis=2, tiled=True)  6.92 us
    dot_general x1, matrix products, body(): jnp.dot(own_normed, kv_weight, preferred_element_type=jnp.float32)  5.63 us
    unnamed x1, blocking collectives  4.85 us
    unnamed x16, local copies, waits for them, and re-layouts  3.85 us
    all_to_all x1, starting transfers between devices, body(): lax.all_to_all(rounded, 'hid', split_axis=0, concat_axis=2, tiled=True)  3.37 us
    psum x1, blocking collectives, body(): lax.psum((jnp.sum(row_values, axis=1), jnp.sum(row_values * row_values, a...  2.47 us
  transfers between devices with their start and end apart: 3, of which 2 were waited for; matrix products, arithmetic and copies ran while one was open for 10% of the time, Pallas kernels for 0%

commit v1 on v0

v1 whole, which is shorter than its diff:
```python
import functools

import jax
import jax.numpy as jnp
from jax import lax
from jax.experimental import pallas as pl
from jax.experimental.pallas import tpu as pltpu
from jax.sharding import PartitionSpec as P

EPSILON = 1e-05
CHUNKS = 6
ROWS_Y = 2
UP, DOWN, SIDE = 0, 1, 2
MESH = pl.DeviceIdType.MESH


def kernel(
    hid_count, wid_count,
    tok_hbm, gain_hbm, qw_hbm, qs_hbm, kw_hbm, ks_hbm, keys_hbm, vals_hbm, len_ref,
    att_ref, new_ref,
    gat, gain, qw, qs, kw, ks, keys, vals,
    stat_mine, stat_other, stats, normed, acc, acc_rx, kv_acc, kv_rx, kv_new,
    q_tx, q_rx, q_f32, o_f32, att,
    tok_sem, qw_sem, kw_sem, misc_sem,
    send_sem, recv_sem, pair_sem, stat_send, stat_recv, acc_send, acc_recv, q_send, q_recv, out_sem,
):
    own_rows, half_width = tok_hbm.shape
    full_width = half_width * wid_count
    width = half_width // CHUNKS
    tiles, _, _, req, head_dim = acc.shape
    z_count = hid_count // ROWS_Y
    me = lax.axis_index("hid")
    core = lax.axis_index("wid")
    other = 1 - core
    z = me // ROWS_Y
    y = lax.rem(me, ROWS_Y)
    side = z * ROWS_Y + (1 - y)

    def hid_at(zz, yy):
        return zz * ROWS_Y + yy

    def cols(c):
        return pl.ds(pl.multiple_of(c * width, 128), width)

    def tok_copy(c):
        return pltpu.make_async_copy(tok_hbm.at[:, cols(c)], gat.at[me, c], tok_sem.at[c])

    def kw_copy(c):
        return pltpu.make_async_copy(kw_hbm.at[cols(c)], kw.at[c], kw_sem.at[c])

    def qw_copy(c):
        return pltpu.make_async_copy(qw_hbm.at[cols(c)], qw.at[c], qw_sem.at[c])

    small = [
        pltpu.make_async_copy(gain_hbm, gain, misc_sem.at[0]),
        pltpu.make_async_copy(qs_hbm, qs, misc_sem.at[1]),
        pltpu.make_async_copy(ks_hbm, ks, misc_sem.at[2]),
        pltpu.make_async_copy(keys_hbm, keys, misc_sem.at[3]),
        pltpu.make_async_copy(vals_hbm, vals, misc_sem.at[4]),
    ]
    for c in range(CHUNKS):
        tok_copy(c).start()
    for copy in small[:3]:
        copy.start()

    barrier = pltpu.get_barrier_semaphore()
    for d in range(1, hid_count):
        pl.semaphore_signal(
            barrier, inc=1, device_id={"hid": lax.rem(me + d, hid_count)}, device_id_type=MESH
        )
    pl.semaphore_signal(barrier, inc=1, device_id={"wid": other}, device_id_type=MESH)
    for c in range(CHUNKS):
        kw_copy(c).start()
    for c in range(CHUNKS):
        qw_copy(c).start()
    for copy in small[3:]:
        copy.start()

    row_sum = jnp.zeros((own_rows, 1), jnp.float32)
    row_squares = jnp.zeros((own_rows, 1), jnp.float32)
    for c in range(CHUNKS):
        tok_copy(c).wait()
        block = gat[me, c].astype(jnp.float32)
        row_sum += jnp.sum(block, axis=1, keepdims=True)
        row_squares += jnp.sum(block * block, axis=1, keepdims=True)
    lane = lax.broadcasted_iota(jnp.int32, (own_rows, 128), 1)
    stat_mine[...] = jnp.where(lane < 64, row_sum, row_squares)

    pl.semaphore_wait(barrier, hid_count)

    def send(h, c, link):
        if link == UP:
            target = hid_at(z + 1, y)
        elif link == DOWN:
            target = hid_at(z - 1, y)
        else:
            target = side
        return pltpu.make_async_remote_copy(
            src_ref=gat.at[h, c], dst_ref=gat.at[h, c],
            send_sem=send_sem.at[link, h, c], recv_sem=recv_sem.at[h, c],
            device_id={"hid": target}, device_id_type=MESH,
        )

    def arrived(h, c):
        pltpu.make_async_remote_copy(
            src_ref=gat.at[h, c], dst_ref=gat.at[h, c],
            send_sem=send_sem.at[SIDE, h, c], recv_sem=recv_sem.at[h, c],
            device_id={"hid": side}, device_id_type=MESH,
        ).wait_recv()

    def pair(src, dst, k):
        return pltpu.make_async_remote_copy(
            src_ref=src, dst_ref=dst, send_sem=pair_sem.at[0, k], recv_sem=pair_sem.at[1, k],
            device_id={"wid": other}, device_id_type=MESH,
        )

    def own_sends(c, act):
        @pl.when(z + 1 < z_count)
        def _():
            act(send(me, c, UP))

        @pl.when(z > 0)
        def _():
            act(send(me, c, DOWN))

        act(send(me, c, SIDE))

    start = lambda copy: copy.start()
    stat_pair = pair(stat_mine, stat_other, 0)
    stat_pair.start()
    own_sends(0, start)
    own_sends(1, start)
    stat_pair.wait()
    both = stat_mine[...] + stat_other[...]
    row_mean = both[:, 0:1] / full_width
    variance = both[:, 64:65] / full_width - row_mean * row_mean
    stats[me] = jnp.where(lane < 64, row_mean, lax.rsqrt(variance + EPSILON))

    def stat_copy(d):
        target = lax.rem(me + d, hid_count)
        return pltpu.make_async_remote_copy(
            src_ref=stats.at[me], dst_ref=stats.at[me],
            send_sem=stat_send.at[d], recv_sem=stat_recv.at[me],
            device_id={"hid": target}, device_id_type=MESH,
        )

    def stat_arrived(h):
        pltpu.make_async_remote_copy(
            src_ref=stats.at[h], dst_ref=stats.at[h],
            send_sem=stat_send.at[0], recv_sem=stat_recv.at[h],
            device_id={"hid": side}, device_id_type=MESH,
        ).wait_recv()

    for d in range(1, hid_count):
        stat_copy(d).start()
    for c in range(2, CHUNKS):
        own_sends(c, start)

    for copy in small[:3]:
        copy.wait()

    def normalised(h, c):
        stat = stats[h]
        block = gat[h, c].astype(jnp.float32)
        return ((block - stat[:, 0:1]) * stat[:, 64:65] * gain[:, cols(c)]).astype(jnp.bfloat16)

    kv_acc[...] = jnp.zeros_like(kv_acc)

    def kv_step(c, carry):
        kw_copy(c).wait()
        part = jnp.dot(normalised(me, c), kw[c], preferred_element_type=jnp.float32)
        kv_acc[...] += part.reshape(kv_acc.shape)
        return carry

    lax.fori_loop(0, CHUNKS, kv_step, 0)
    kv_pair = pair(kv_acc.at[other], kv_rx, 1)
    kv_pair.start()

    acc[...] = jnp.zeros_like(acc)

    def for_sources(visit):
        for k in range(1, z_count):
            @pl.when(z - k >= 0)
            def _():
                visit(z - k, UP)

            @pl.when(z + k < z_count)
            def _():
                visit(z + k, DOWN)

    def onward(h, c, link, act):
        if link == UP:
            @pl.when(z + 1 < z_count)
            def _():
                act(send(h, c, UP))
        else:
            @pl.when(z > 0)
            def _():
                act(send(h, c, DOWN))

    def relay(c, act, wait):
        def visit(zz, link):
            h = hid_at(zz, y)
            if wait:
                arrived(h, c)
            onward(h, c, link, act)
            act(send(h, c, SIDE))

        for_sources(visit)

    def relay_last(c, act, wait):
        if wait:
            arrived(side, c)
        onward(side, c, UP, act)
        onward(side, c, DOWN, act)

        def visit(zz, link):
            for yy in (y, 1 - y):
                h = hid_at(zz, yy)
                if wait:
                    arrived(h, c)
                onward(h, c, link, act)

        for_sources(visit)

    def arrived_side(c):
        arrived(side, c)

        def visit(zz, link):
            arrived(hid_at(zz, 1 - y), c)

        for_sources(visit)

    def normalise_all(c):
        def one(h, carry):
            normed[pl.ds(pl.multiple_of(h * own_rows, own_rows), own_rows), :] = normalised(h, c)
            return carry

        lax.fori_loop(0, hid_count, one, 0)

    def product(c, n):
        columns = pl.ds(n * head_dim, head_dim)
        part = jnp.dot(normed[...], qw[c, :, columns], preferred_element_type=jnp.float32)
        return part.reshape(acc.shape[1:])

    def compute(c):
        normalise_all(c)
        qw_copy(c).wait()
        for n in range(tiles):
            acc[n] += product(c, n)

    last = CHUNKS - 1
    relay(0, start, True)
    for d in range(1, hid_count):
        stat_arrived(lax.rem(me + d, hid_count))

    def step(c, carry):
        relay(c, start, True)
        arrived_side(c - 1)
        compute(c - 1)
        return carry

    lax.fori_loop(1, last, step, 0)
    kv_pair.wait()
    kv_new[...] = ((kv_acc[core] + kv_rx[...]) * ks[...]).astype(jnp.bfloat16)
    new_out = pltpu.make_async_copy(kv_new, new_ref, out_sem.at[0])
    new_out.start()
    relay_last(last, start, True)
    arrived_side(last - 1)
    compute(last - 1)

    def acc_copy(n):
        return pltpu.make_async_remote_copy(
            src_ref=acc.at[n, :, other], dst_ref=acc_rx.at[n],
            send_sem=acc_send.at[n], recv_sem=acc_recv.at[n],
            device_id={"wid": other}, device_id_type=MESH,
        )

    def q_copy(n, d):
        target = lax.rem(me + d, hid_count)
        return pltpu.make_async_remote_copy(
            src_ref=q_tx.at[n, target], dst_ref=q_rx.at[me * tiles + n],
            send_sem=q_send.at[n, d], recv_sem=q_recv.at[me * tiles + n],
            device_id={"hid": target}, device_id_type=MESH,
        )

    def q_arrived(h, n):
        pltpu.make_async_remote_copy(
            src_ref=q_tx.at[n, h], dst_ref=q_rx.at[h * tiles + n],
            send_sem=q_send.at[n, 0], recv_sem=q_recv.at[h * tiles + n],
            device_id={"hid": side}, device_id_type=MESH,
        ).wait_recv()

    normalise_all(last)
    qw_copy(last).wait()
    for n in range(tiles):
        acc[n] += product(last, n)
        acc_copy(n).start()
    for n in range(tiles):
        acc_copy(n).wait_recv()
        total = acc[n, :, core] + acc_rx[n]
        scale = qs[:, pl.ds(n * head_dim, head_dim)]
        q_tx[n] = (total * scale[None]).astype(jnp.bfloat16)
        for d in range(1, hid_count):
            q_copy(n, d).start()
        q_rx[me * tiles + n] = q_tx[n, me]

    finish = lambda copy: copy.wait_send()

    def drain(c, carry):
        own_sends(c, finish)
        return carry

    lax.fori_loop(0, CHUNKS, drain, 0)

    def drain_relay(c, carry):
        relay(c, finish, False)
        return carry

    lax.fori_loop(0, last, drain_relay, 0)
    relay_last(last, finish, False)
    for d in range(1, hid_count):
        stat_copy(d).wait_send()
    for copy in small[3:]:
        copy.wait()

    for n in range(tiles):
        for d in range(1, hid_count):
            q_arrived(lax.rem(me + d, hid_count), n)

    heads = hid_count * tiles
    cache_len = keys.shape[1]
    inv_root = head_dim ** (-0.5)
    q_f32[...] = q_rx[...].astype(jnp.float32)
    position = lax.broadcasted_iota(jnp.int32, (heads, cache_len), 1)
    entries = kv_new[...].astype(jnp.float32)
    for r in range(req):
        query = q_f32[:, r, :]
        score = lax.dot_general(
            query.astype(jnp.bfloat16), keys[r], (((1,), (1,)), ((), ())),
            preferred_element_type=jnp.float32,
        ) * inv_root
        score = jnp.where(position < len_ref[r], score, -jnp.inf)
        own = jnp.sum(query * entries[r : r + 1, :head_dim], axis=1, keepdims=True) * inv_root
        peak = jnp.maximum(jnp.max(score, axis=1, keepdims=True), own)
        weight = jnp.exp(score - peak)
        own_weight = jnp.exp(own - peak)
        denom = jnp.sum(weight, axis=1, keepdims=True) + own_weight
        weight = (weight / denom).astype(jnp.bfloat16)
        own_weight = (own_weight / denom).astype(jnp.bfloat16).astype(jnp.float32)
        mixed = jnp.dot(weight, vals[r], preferred_element_type=jnp.float32)
        o_f32[:, r, :] = mixed + own_weight * entries[r : r + 1, head_dim:]
    for h in range(heads):
        att[:, h * head_dim : (h + 1) * head_dim] = o_f32[h].astype(jnp.bfloat16)
    att_out = pltpu.make_async_copy(att, att_ref, out_sem.at[1])
    att_out.start()
    for n in range(tiles):
        acc_copy(n).wait_send()
        for d in range(1, hid_count):
            q_copy(n, d).wait_send()
    new_out.wait()
    att_out.wait()


def body(
    tokens, norm_gain, query_weight, query_scale, kv_weight, kv_scale,
    keys_cache, values_cache, lengths,
):
    hid_count = lax.axis_size("hid")
    wid_count = lax.axis_size("wid")
    own_rows, half_width = tokens.shape
    local_cols = query_weight.shape[1]
    req, cache_len, head_dim = keys_cache.shape
    tiles = local_cols // head_dim
    heads = hid_count * tiles
    width = half_width // CHUNKS
    kv_cols = kv_weight.shape[1]
    bf16, f32 = jnp.bfloat16, jnp.float32
    dma = pltpu.SemaphoreType.DMA
    vm = pltpu.VMEM
    scratch = [
        vm((hid_count, CHUNKS, own_rows, width), bf16),
        vm((1, half_width), f32),
        vm((CHUNKS, width, local_cols), bf16),
        vm((1, local_cols), f32),
        vm((CHUNKS, width, kv_cols), bf16),
        vm((1, kv_cols), f32),
        vm(keys_cache.shape, bf16),
        vm(values_cache.shape, bf16),
        vm((own_rows, 128), f32),
        vm((own_rows, 128), f32),
        vm((hid_count, own_rows, 128), f32),
        vm((hid_count * own_rows, width), bf16),
        vm((tiles, hid_count, wid_count, req, head_dim), f32),
        vm((tiles, hid_count, req, head_dim), f32),
        vm((wid_count, req, kv_cols), f32),
        vm((req, kv_cols), f32),
        vm((req, kv_cols), bf16),
        vm((tiles, hid_count, req, head_dim), bf16),
        vm((heads, req, head_dim), bf16),
        vm((heads, req, head_dim), f32),
        vm((heads, req, head_dim), f32),
        vm((req, heads * head_dim), bf16),
        dma((CHUNKS,)),
        dma((CHUNKS,)),
        dma((CHUNKS,)),
        dma((5,)),
        dma((3, hid_count, CHUNKS)),
        dma((hid_count, CHUNKS)),
        dma((2, 2)),
        dma((hid_count,)),
        dma((hid_count,)),
        dma((tiles,)),
        dma((tiles,)),
        dma((tiles, hid_count)),
        dma((heads,)),
        dma((2,)),
    ]
    hbm = pl.BlockSpec(memory_space=pl.ANY)
    return pl.pallas_call(
        functools.partial(kernel, hid_count, wid_count),
        out_shape=(
            jax.ShapeDtypeStruct((req, heads * head_dim), bf16),
            jax.ShapeDtypeStruct((req, kv_cols), bf16),
        ),
        in_specs=[hbm] * 8 + [pl.BlockSpec(memory_space=pltpu.SMEM)],
        out_specs=(hbm, hbm),
        scratch_shapes=scratch,
        compiler_params=pltpu.CompilerParams(
            collective_id=0, has_side_effects=True, vmem_limit_bytes=60 * 1024 * 1024
        ),
    )(
        tokens, norm_gain.reshape(1, -1), query_weight, query_scale.reshape(1, -1),
        kv_weight, kv_scale.reshape(1, -1), keys_cache, values_cache, lengths,
    )


def solution(mesh):
    placed = (
        P(("groups", "hid"), "wid"),
        P("wid"),
        P("wid", "hid"),
        P("hid"),
        P("wid", None),
        P(),
        P(("groups", "hid", "wid"), None, None),
        P(("groups", "hid", "wid"), None, None),
        P(("groups", "hid", "wid")),
    )
    return jax.shard_map(
        body,
        mesh=mesh,
        in_specs=placed,
        out_specs=(P(("groups", "hid", "wid"), None), P(("groups", "hid", "wid"), None)),
        check_vma=False,
    )
```

time: 115 us -> 66.6 us (0.58)
  waiting for transfers between devices: 63.1 us -> 0 us
  Pallas kernels: 0 us -> 62.8 us
  matrix products: 15.6 us -> 0 us
  between operations: 14.2 us -> 0.64 us
  blocking collectives: 7.32 us -> 0 us
  other arithmetic: 5.88 us -> 0 us
  starting transfers between devices: 3.45 us -> 0 us
  local copies, waits for them, and re-layouts: 5.37 us -> 2.86 us
    pallas_call x0 -> x1, Pallas kernels: none -> 62.8 us  [body(): pl.pallas_call(functools.partial(kernel, hid_count, wid_count), out_shape...]
    all_gather x1 -> x0, waiting for transfers between devices: 55.5 us -> none  [body(): gathered = lax.all_gather(tokens, 'hid', axis=0, tiled=True)]
    dot_general x5 -> x0, matrix products: 15.6 us -> none  [the longest x1 8.51 us: body(): jnp.dot(all_normed, query_weight, preferred_element_type=jnp.float32)]
    all_to_all x1 -> x0, waiting for transfers between devices: 6.92 us -> none  [body(): lax.all_to_all(rounded, 'hid', split_axis=0, concat_axis=2, tiled=True)]
    unnamed x1 -> x0, blocking collectives: 4.85 us -> none
    all_to_all x1 -> x0, starting transfers between devices: 3.37 us -> none  [body(): lax.all_to_all(rounded, 'hid', split_axis=0, concat_axis=2, tiled=True)]
    convert_element_type x3 -> x0, other arithmetic: 3.17 us -> none  [the longest x1 2.46 us: layer_norm(): return ((row_values - row_mean[:, None]) * lax.rsqrt(variance + EPSILON)[...]
    reduce_sum x2 -> x0, other arithmetic: 2.61 us -> none  [the longest x1 2.38 us: body(): jnp.sum(row_values, axis=1)]
  transfers between devices with their start and end apart: 3 -> 0, of which waited for: 2 -> 0; matrix products, arithmetic and copies ran while one was open for 10% -> 0% of each run, Pallas kernels for 0% -> 0%
where the time goes in v1:
time: 66.6 us; the launch traced here: 66.3 us
  Pallas kernels  62.8 us (94%)
  local copies, waits for them, and re-layouts  2.86 us (4%)
    pallas_call x1, Pallas kernels, body(): pl.pallas_call(functools.partial(kernel, hid_count, wid_count), out_shape...  62.8 us
    unnamed x2, local copies, waits for them, and re-layouts  2.86 us

profile of v1, /device:TPU:0, one launch (start us, length us, event | category | flops | bytes accessed | tf_op | source)
XLA Modules:
  0.0 66.3 jit_solution(18442931412626376500)
XLA Ops:
  0.6 62.8 %shard_map.104 = (bf16[8,8192]{1,0:T(8,128)(2,1)}, bf16[8,512]{1,0:T(8,128)(2,1)}) custom-call(bf16[16,9216]{1,0:T(8,128)(2,1)} %tok_hbm.1, f32[1,9216]{1,0:T(1,128)} %bitcast.3, bf16[9216,1024]{1,0:T(8,128)(2,1)} %qw_hbm.1, f32[1,1024]{1,0:T(1,128)} %bitcast.4, bf16[9216,512]{1,0:T(8,128)(2,1)} %kw_hbm.1, f32[1,512]{1,0:T(1,128)} %bitcast.5, ...), custom_call_target="tpu_custom_call" | custom-call | tf_op jit(solution)/shard_map/pallas_call | solution.py:420
  63.5 1.6 %copy.13 = bf16[8,8192]{1,0:T(8,128)(2,1)} copy(bf16[8,8192]{1,0:T(8,128)(2,1)} %get-tuple-element.4) | data formatting | bytes 262144
  65.0 1.3 %copy.14 = bf16[8,512]{1,0:T(8,128)(2,1)} copy(bf16[8,512]{1,0:T(8,128)(2,1)} %get-tuple-element.5) | data formatting | bytes 16384

commit v2 on v1

--- a/solution.py
+++ b/solution.py
@@ -22,7 +22,7 @@
     stat_mine, stat_other, stats, normed, acc, acc_rx, kv_acc, kv_rx, kv_new,
     q_tx, q_rx, q_f32, o_f32, att,
     tok_sem, qw_sem, kw_sem, misc_sem,
-    send_sem, recv_sem, pair_sem, stat_send, stat_recv, acc_send, acc_recv, q_send, q_recv, out_sem,
+    send_sem, recv_sem, pair_sem, acc_send, acc_recv, q_send, q_recv, out_sem,
 ):
     own_rows, half_width = tok_hbm.shape
     full_width = half_width * wid_count
@@ -64,10 +64,16 @@
         copy.start()
 
     barrier = pltpu.get_barrier_semaphore()
-    for d in range(1, hid_count):
-        pl.semaphore_signal(
-            barrier, inc=1, device_id={"hid": lax.rem(me + d, hid_count)}, device_id_type=MESH
-        )
+
+    @pl.when(z + 1 < z_count)
+    def _():
+        pl.semaphore_signal(barrier, inc=1, device_id={"hid": hid_at(z + 1, y)}, device_id_type=MESH)
+
+    @pl.when(z > 0)
+    def _():
+        pl.semaphore_signal(barrier, inc=1, device_id={"hid": hid_at(z - 1, y)}, device_id_type=MESH)
+
+    pl.semaphore_signal(barrier, inc=1, device_id={"hid": side}, device_id_type=MESH)
     pl.semaphore_signal(barrier, inc=1, device_id={"wid": other}, device_id_type=MESH)
     for c in range(CHUNKS):
         kw_copy(c).start()
@@ -75,6 +81,55 @@
         qw_copy(c).start()
     for copy in small[3:]:
         copy.start()
+
+    def block_at(h, c):
+        return stats.at[h] if isinstance(c, int) and c == CHUNKS else gat.at[h, c]
+
+    def send(h, c, link, src=None):
+        if link == UP:
+            target = hid_at(z + 1, y)
+        elif link == DOWN:
+            target = hid_at(z - 1, y)
+        else:
+            target = side
+        place = block_at(h, c)
+        return pltpu.make_async_remote_copy(
+            src_ref=place if src is None else src, dst_ref=place,
+            send_sem=send_sem.at[link, h, c], recv_sem=recv_sem.at[h, c],
+            device_id={"hid": target}, device_id_type=MESH,
+        )
+
+    def arrived(h, c):
+        pltpu.make_async_remote_copy(
+            src_ref=block_at(h, c), dst_ref=block_at(h, c),
+            send_sem=send_sem.at[SIDE, h, c], recv_sem=recv_sem.at[h, c],
+            device_id={"hid": side}, device_id_type=MESH,
+        ).wait_recv()
+
+    def pair(src, dst, k):
+        return pltpu.make_async_remote_copy(
+            src_ref=src, dst_ref=dst, send_sem=pair_sem.at[0, k], recv_sem=pair_sem.at[1, k],
+            device_id={"wid": other}, device_id_type=MESH,
+        )
+
+    def own_sends(c, act):
+        src = stats.at[me] if isinstance(c, int) and c == CHUNKS else tok_hbm.at[:, cols(c)]
+
+        @pl.when(z + 1 < z_count)
+        def _():
+            act(send(me, c, UP, src))
+
+        @pl.when(z > 0)
+        def _():
+            act(send(me, c, DOWN, src))
+
+        act(send(me, c, SIDE, src))
+
+    start = lambda copy: copy.start()
+    ends = (z == 0).astype(jnp.int32) + (z == z_count - 1).astype(jnp.int32)
+    pl.semaphore_wait(barrier, 4 - ends)
+    own_sends(0, start)
+    own_sends(1, start)
 
     row_sum = jnp.zeros((own_rows, 1), jnp.float32)
     row_squares = jnp.zeros((own_rows, 1), jnp.float32)
@@ -86,73 +141,14 @@
     lane = lax.broadcasted_iota(jnp.int32, (own_rows, 128), 1)
     stat_mine[...] = jnp.where(lane < 64, row_sum, row_squares)
 
-    pl.semaphore_wait(barrier, hid_count)
-
-    def send(h, c, link):
-        if link == UP:
-            target = hid_at(z + 1, y)
-        elif link == DOWN:
-            target = hid_at(z - 1, y)
-        else:
-            target = side
-        return pltpu.make_async_remote_copy(
-            src_ref=gat.at[h, c], dst_ref=gat.at[h, c],
-            send_sem=send_sem.at[link, h, c], recv_sem=recv_sem.at[h, c],
-            device_id={"hid": target}, device_id_type=MESH,
-        )
-
-    def arrived(h, c):
-        pltpu.make_async_remote_copy(
-            src_ref=gat.at[h, c], dst_ref=gat.at[h, c],
-            send_sem=send_sem.at[SIDE, h, c], recv_sem=recv_sem.at[h, c],
-            device_id={"hid": side}, device_id_type=MESH,
-        ).wait_recv()
-
-    def pair(src, dst, k):
-        return pltpu.make_async_remote_copy(
-            src_ref=src, dst_ref=dst, send_sem=pair_sem.at[0, k], recv_sem=pair_sem.at[1, k],
-            device_id={"wid": other}, device_id_type=MESH,
-        )
-
-    def own_sends(c, act):
-        @pl.when(z + 1 < z_count)
-        def _():
-            act(send(me, c, UP))
-
-        @pl.when(z > 0)
-        def _():
-            act(send(me, c, DOWN))
-
-        act(send(me, c, SIDE))
-
-    start = lambda copy: copy.start()
     stat_pair = pair(stat_mine, stat_other, 0)
     stat_pair.start()
-    own_sends(0, start)
-    own_sends(1, start)
     stat_pair.wait()
     both = stat_mine[...] + stat_other[...]
     row_mean = both[:, 0:1] / full_width
     variance = both[:, 64:65] / full_width - row_mean * row_mean
     stats[me] = jnp.where(lane < 64, row_mean, lax.rsqrt(variance + EPSILON))
-
-    def stat_copy(d):
-        target = lax.rem(me + d, hid_count)
-        return pltpu.make_async_remote_copy(
-            src_ref=stats.at[me], dst_ref=stats.at[me],
-            send_sem=stat_send.at[d], recv_sem=stat_recv.at[me],
-            device_id={"hid": target}, device_id_type=MESH,
-        )
-
-    def stat_arrived(h):
-        pltpu.make_async_remote_copy(
-            src_ref=stats.at[h], dst_ref=stats.at[h],
-            send_sem=stat_send.at[0], recv_sem=stat_recv.at[h],
-            device_id={"hid": side}, device_id_type=MESH,
-        ).wait_recv()
-
-    for d in range(1, hid_count):
-        stat_copy(d).start()
+    own_sends(CHUNKS, start)
     for c in range(2, CHUNKS):
         own_sends(c, start)
 
@@ -178,15 +174,18 @@
 
     acc[...] = jnp.zeros_like(acc)
 
+    def sources_at(k, visit):
+        @pl.when(z - k >= 0)
+        def _():
+            visit(z - k, UP)
+
+        @pl.when(z + k < z_count)
+        def _():
+            visit(z + k, DOWN)
+
     def for_sources(visit):
         for k in range(1, z_count):
-            @pl.when(z - k >= 0)
-            def _():
-                visit(z - k, UP)
-
-            @pl.when(z + k < z_count)
-            def _():
-                visit(z + k, DOWN)
+            sources_at(k, visit)
 
     def onward(h, c, link, act):
         if link == UP:
@@ -198,7 +197,7 @@
             def _():
                 act(send(h, c, DOWN))
 
-    def relay(c, act, wait):
+    def relay_at(k, c, act, wait):
         def visit(zz, link):
             h = hid_at(zz, y)
             if wait:
@@ -206,14 +205,15 @@
             onward(h, c, link, act)
             act(send(h, c, SIDE))
 
-        for_sources(visit)
-
-    def relay_last(c, act, wait):
+        sources_at(k, visit)
+
+    def relay_last_side(c, act, wait):
         if wait:
             arrived(side, c)
         onward(side, c, UP, act)
         onward(side, c, DOWN, act)
 
+    def relay_last_at(k, c, act, wait):
         def visit(zz, link):
             for yy in (y, 1 - y):
                 h = hid_at(zz, yy)
@@ -221,7 +221,7 @@
                     arrived(h, c)
                 onward(h, c, link, act)
 
-        for_sources(visit)
+        sources_at(k, visit)
 
     def arrived_side(c):
         arrived(side, c)
@@ -239,35 +239,47 @@
         lax.fori_loop(0, hid_count, one, 0)
 
     def product(c, n):
-        columns = pl.ds(n * head_dim, head_dim)
+        columns = pl.ds(pl.multiple_of(n * head_dim, head_dim), head_dim)
         part = jnp.dot(normed[...], qw[c, :, columns], preferred_element_type=jnp.float32)
         return part.reshape(acc.shape[1:])
 
     def compute(c):
         normalise_all(c)
         qw_copy(c).wait()
-        for n in range(tiles):
+
+        def one(n, carry):
             acc[n] += product(c, n)
+            return carry
+
+        lax.fori_loop(0, tiles, one, 0)
 
     last = CHUNKS - 1
-    relay(0, start, True)
-    for d in range(1, hid_count):
-        stat_arrived(lax.rem(me + d, hid_count))
-
-    def step(c, carry):
-        relay(c, start, True)
-        arrived_side(c - 1)
-        compute(c - 1)
-        return carry
-
-    lax.fori_loop(1, last, step, 0)
-    kv_pair.wait()
-    kv_new[...] = ((kv_acc[core] + kv_rx[...]) * ks[...]).astype(jnp.bfloat16)
-    new_out = pltpu.make_async_copy(kv_new, new_ref, out_sem.at[0])
-    new_out.start()
-    relay_last(last, start, True)
-    arrived_side(last - 1)
-    compute(last - 1)
+    final = last + z_count - 2
+    for step in range(final + 1):
+        done = step - (z_count - 1)
+        if step == final:
+            arrived_side(done)
+            compute(done)
+        if step < z_count - 1:
+            relay_at(step + 1, CHUNKS, start, True)
+        for k in range(1, z_count):
+            c = step - (k - 1)
+            if 0 <= c < last:
+                relay_at(k, c, start, True)
+            elif c == last:
+                relay_last_at(k, c, start, True)
+        if step == min(2, last - 1):
+            relay_last_side(last, start, True)
+        if step == z_count - 2:
+            arrived_side(CHUNKS)
+        if 0 <= done < last - 1:
+            arrived_side(done)
+            compute(done)
+        if step == z_count - 1:
+            kv_pair.wait()
+            kv_new[...] = ((kv_acc[core] + kv_rx[...]) * ks[...]).astype(jnp.bfloat16)
+            new_out = pltpu.make_async_copy(kv_new, new_ref, out_sem.at[0])
+            new_out.start()
 
     def acc_copy(n):
         return pltpu.make_async_remote_copy(
@@ -312,15 +324,18 @@
         return carry
 
     lax.fori_loop(0, CHUNKS, drain, 0)
+    own_sends(CHUNKS, finish)
 
     def drain_relay(c, carry):
-        relay(c, finish, False)
+        for k in range(1, z_count):
+            relay_at(k, c, finish, False)
         return carry
 
     lax.fori_loop(0, last, drain_relay, 0)
-    relay_last(last, finish, False)
-    for d in range(1, hid_count):
-        stat_copy(d).wait_send()
+    relay_last_side(last, finish, False)
+    for k in range(1, z_count):
+        relay_at(k, CHUNKS, finish, False)
+        relay_last_at(k, last, finish, False)
     for copy in small[3:]:
         copy.wait()
 
@@ -405,11 +420,9 @@
         dma((CHUNKS,)),
         dma((CHUNKS,)),
         dma((5,)),
-        dma((3, hid_count, CHUNKS)),
-        dma((hid_count, CHUNKS)),
+        dma((3, hid_count, CHUNKS + 1)),
+        dma((hid_count, CHUNKS + 1)),
         dma((2, 2)),
-        dma((hid_count,)),
-        dma((hid_count,)),
         dma((tiles,)),
         dma((tiles,)),
         dma((tiles, hid_count)),

time: 66.6 us -> 55.5 us (0.83)
  Pallas kernels: 62.8 us -> 51.8 us
    pallas_call x1, Pallas kernels: 62.8 us -> 51.8 us  [body(): pl.pallas_call(functools.partial(kernel, hid_count, wid_count), out_shape...]
where the time goes in v2:
time: 55.5 us; the launch traced here: 55.3 us
  Pallas kernels  51.8 us (93%)
  local copies, waits for them, and re-layouts  2.86 us (5%)
  between operations  0.64 us (1%)
    pallas_call x1, Pallas kernels, body(): pl.pallas_call(functools.partial(kernel, hid_count, wid_count), out_shape...  51.8 us
    unnamed x2, local copies, waits for them, and re-layouts  2.86 us

profile of v2, /device:TPU:0, one launch (start us, length us, event | category | flops | bytes accessed | tf_op | source)
XLA Modules:
  0.0 55.3 jit_solution(14037194955205863641)
XLA Ops:
  0.6 51.8 %shard_map.104 = (bf16[8,8192]{1,0:T(8,128)(2,1)}, bf16[8,512]{1,0:T(8,128)(2,1)}) custom-call(bf16[16,9216]{1,0:T(8,128)(2,1)} %tok_hbm.1, f32[1,9216]{1,0:T(1,128)} %bitcast.3, bf16[9216,1024]{1,0:T(8,128)(2,1)} %qw_hbm.1, f32[1,1024]{1,0:T(1,128)} %bitcast.4, bf16[9216,512]{1,0:T(8,128)(2,1)} %kw_hbm.1, f32[1,512]{1,0:T(1,128)} %bitcast.5, ...), custom_call_target="tpu_custom_call" | custom-call | tf_op jit(solution)/shard_map/pallas_call | solution.py:433
  52.4 1.6 %copy.13 = bf16[8,8192]{1,0:T(8,128)(2,1)} copy(bf16[8,8192]{1,0:T(8,128)(2,1)} %get-tuple-element.4) | data formatting | bytes 262144
  54.0 1.3 %copy.14 = bf16[8,512]{1,0:T(8,128)(2,1)} copy(bf16[8,512]{1,0:T(8,128)(2,1)} %get-tuple-element.5) | data formatting | bytes 16384

commit v3 on v2

--- a/solution.py
+++ b/solution.py
@@ -8,7 +8,7 @@
 from jax.sharding import PartitionSpec as P
 
 EPSILON = 1e-05
-CHUNKS = 6
+CHUNKS = 4
 ROWS_Y = 2
 UP, DOWN, SIDE = 0, 1, 2
 MESH = pl.DeviceIdType.MESH
@@ -128,8 +128,8 @@
     start = lambda copy: copy.start()
     ends = (z == 0).astype(jnp.int32) + (z == z_count - 1).astype(jnp.int32)
     pl.semaphore_wait(barrier, 4 - ends)
-    own_sends(0, start)
-    own_sends(1, start)
+    for c in range(CHUNKS):
+        own_sends(c, start)
 
     row_sum = jnp.zeros((own_rows, 1), jnp.float32)
     row_squares = jnp.zeros((own_rows, 1), jnp.float32)
@@ -149,8 +149,6 @@
     variance = both[:, 64:65] / full_width - row_mean * row_mean
     stats[me] = jnp.where(lane < 64, row_mean, lax.rsqrt(variance + EPSILON))
     own_sends(CHUNKS, start)
-    for c in range(2, CHUNKS):
-        own_sends(c, start)
 
     for copy in small[:3]:
         copy.wait()
@@ -168,10 +166,7 @@
         kv_acc[...] += part.reshape(kv_acc.shape)
         return carry
 
-    lax.fori_loop(0, CHUNKS, kv_step, 0)
     kv_pair = pair(kv_acc.at[other], kv_rx, 1)
-    kv_pair.start()
-
     acc[...] = jnp.zeros_like(acc)
 
     def sources_at(k, visit):
@@ -260,8 +255,6 @@
         if step == final:
             arrived_side(done)
             compute(done)
-        if step < z_count - 1:
-            relay_at(step + 1, CHUNKS, start, True)
         for k in range(1, z_count):
             c = step - (k - 1)
             if 0 <= c < last:
@@ -270,12 +263,18 @@
                 relay_last_at(k, c, start, True)
         if step == min(2, last - 1):
             relay_last_side(last, start, True)
-        if step == z_count - 2:
+        if step < CHUNKS // 2:
+            lax.fori_loop(2 * step, 2 * step + 2, kv_step, 0)
+        if step == CHUNKS // 2 - 1:
+            kv_pair.start()
+        if 1 <= step < z_count:
+            relay_at(step, CHUNKS, start, True)
+        if step == z_count - 1:
             arrived_side(CHUNKS)
         if 0 <= done < last - 1:
             arrived_side(done)
             compute(done)
-        if step == z_count - 1:
+        if step == max(z_count - 1, CHUNKS // 2):
             kv_pair.wait()
             kv_new[...] = ((kv_acc[core] + kv_rx[...]) * ks[...]).astype(jnp.bfloat16)
             new_out = pltpu.make_async_copy(kv_new, new_ref, out_sem.at[0])
@@ -375,6 +374,11 @@
             q_copy(n, d).wait_send()
     new_out.wait()
     att_out.wait()
+
+
+def hand_on(att_ref, new_ref, att_out, new_out):
+    att_out[...] = att_ref[...]
+    new_out[...] = new_ref[...]
 
 
 def body(
@@ -430,7 +434,7 @@
         dma((2,)),
     ]
     hbm = pl.BlockSpec(memory_space=pl.ANY)
-    return pl.pallas_call(
+    attended, new_entries = pl.pallas_call(
         functools.partial(kernel, hid_count, wid_count),
         out_shape=(
             jax.ShapeDtypeStruct((req, heads * head_dim), bf16),
@@ -446,6 +450,16 @@
         tokens, norm_gain.reshape(1, -1), query_weight, query_scale.reshape(1, -1),
         kv_weight, kv_scale.reshape(1, -1), keys_cache, values_cache, lengths,
     )
+    whole = pl.BlockSpec(memory_space=pltpu.VMEM)
+    return pl.pallas_call(
+        hand_on,
+        out_shape=(
+            jax.ShapeDtypeStruct(attended.shape, bf16),
+            jax.ShapeDtypeStruct(new_entries.shape, bf16),
+        ),
+        in_specs=[whole, whole],
+        out_specs=(whole, whole),
+    )(attended, new_entries)
 
 
 def solution(mesh):

time: 55.5 us -> 52.7 us (0.950)
  local copies, waits for them, and re-layouts: 2.86 us -> 0 us
    unnamed x2 -> x0, local copies, waits for them, and re-layouts: 2.86 us -> none
    pallas_call x0 -> x1, Pallas kernels: none -> 1.57 us  [body(): pl.pallas_call(hand_on, out_shape=(jax.ShapeDtypeStruct(attended.shape, b...]
    pallas_call x1, Pallas kernels: 51.8 us -> 50.3 us  [body(): pl.pallas_call(functools.partial(kernel, hid_count, wid_count), out_shape...]
where the time goes in v3:
time: 52.7 us; the launch traced here: 52.6 us
  Pallas kernels  51.9 us (98%)
  between operations  0.64 us (1%)
    pallas_call x1, Pallas kernels, body(): pl.pallas_call(functools.partial(kernel, hid_count, wid_count), out_shape...  50.3 us
    pallas_call x1, Pallas kernels, body(): pl.pallas_call(hand_on, out_shape=(jax.ShapeDtypeStruct(attended.shape, b...  1.57 us

profile of v3, /device:TPU:0, one launch (start us, length us, event | category | flops | bytes accessed | tf_op | source)
XLA Modules:
  0.0 52.6 jit_solution(12856662076931933499)
XLA Ops:
  0.6 50.3 %shard_map.104 = (bf16[8,8192]{1,0:T(8,128)(2,1)}, bf16[8,512]{1,0:T(8,128)(2,1)}) custom-call(bf16[16,9216]{1,0:T(8,128)(2,1)} %tok_hbm.1, f32[1,9216]{1,0:T(1,128)} %bitcast.3, bf16[9216,1024]{1,0:T(8,128)(2,1)} %qw_hbm.1, f32[1,1024]{1,0:T(1,128)} %bitcast.4, bf16[9216,512]{1,0:T(8,128)(2,1)} %kw_hbm.1, f32[1,512]{1,0:T(1,128)} %bitcast.5, ...), custom_call_target="tpu_custom_call" | custom-call | tf_op jit(solution)/shard_map/pallas_call | solution.py:437
  51.0 1.6 %shard_map.105 = (bf16[8,8192]{1,0:T(8,128)(2,1)}, bf16[8,512]{1,0:T(8,128)(2,1)}) custom-call(bf16[8,8192]{1,0:T(8,128)(2,1)} %get-tuple-element.4.att_ref, bf16[8,512]{1,0:T(8,128)(2,1)} %get-tuple-element.5.new_ref), custom_call_target="tpu_custom_call" | custom-call | tf_op jit(solution)/shard_map/pallas_call | solution.py:454
